TPU v7x, 256 devices: a whole 4x4x8 slice. The times are simulated.
256 devices in a mesh: row: 8 (over z), col: 32 (over x, y, core).
Axes of the slice: x: 4, y: 4, z: 8, core: 2. Of those that a mesh axis runs over, the one named last changes fastest.
Arguments:
- a_trail: float32 [16384, 16384], P('row', 'col'), may hold values from -60 to 60, as said below
- a_panel: float32 [16384, 256], P(('row', 'col')), may hold values from -6 to 6
- l_panel: float32 [16384, 256], P(('row', 'col')), may hold values from -0.5 to 0.5
- a_diag: float32 [256, 256], replicated, may hold values from -60 to 60, as said below
- l_inverse: float32 [256, 256], replicated, may hold values from -4 to 4, as said below
Outputs:
- trail_out: float32 [16384, 16384], P('row', 'col')
- panel_out: float32 [16384, 256], P(('row', 'col'))
Inputs may be any that keep to these rules, and one draw needn't show every extreme that they name: `a_trail`: symmetric. `a_diag`: symmetric. `l_inverse`: lower triangular with a positive diagonal.
All inputs are finite; a program needn't handle non-finite values.
Results may differ from a plain program's by a relative error of at most 0.0003.
Values sent between devices are 32-bit elements; how exact they have to be, the bound alone decides.
No kernel may reach another device: no remote copies, remote signals or barrier semaphores. Data moves between devices by JAX's collectives and lax.ppermute only.
A program may use at most 64 MiB of HBM per device.

v0:
```python
import jax
import jax.numpy as jnp
from jax import lax
from jax.sharding import PartitionSpec as P

NS_STEPS = 8
ROWS = 8
COLS = 32
BOTH = ("row", "col")


def product(left, right):
    return jnp.dot(left, right, precision=lax.Precision.HIGHEST, preferred_element_type=jnp.float32)


def product3(left, right):
    return jnp.dot(left, right, precision=lax.Precision.HIGH, preferred_element_type=jnp.float32)


def right_solve(factor, values):
    return lax.linalg.triangular_solve(
        factor, values, left_side=False, lower=True, transpose_a=True
    )


def newton_inverse_of_shifted(top):
    size = top.shape[0]
    residual = -top
    approx = jnp.eye(size, dtype=jnp.float32) + residual
    for step in range(1, NS_STEPS):
        residual = product(residual, residual)
        approx = approx + product(approx, residual)
    return approx


def share(block, axis, size):
    parts = lax.all_to_all(jnp.tile(block, (size, 1)), axis, 0, 0, tiled=True)
    return parts.reshape((size,) + block.shape)


def gather_small(block, axis, size):
    return share(block, axis, size).reshape(size * block.shape[0], block.shape[1])


def scatter_sum(block, axis, size):
    parts = lax.all_to_all(block, axis, 0, 0, tiled=True)
    return jnp.sum(parts.reshape(size, block.shape[0] // size, block.shape[1]), axis=0)


def to_columns(block):
    return lax.ppermute(block, BOTH, [(at, at % 8 * COLS + at // 8) for at in range(ROWS * COLS)])


def to_panel(block):
    return lax.ppermute(block, BOTH, [(at % 8 * COLS + at // 8, at) for at in range(ROWS * COLS)])


def scatter_from_first_row(block):
    size = block.shape[0] // ROWS
    total = jnp.where(lax.axis_index("row") == 0, block[:size], 0.0)
    for at in range(1, ROWS):
        total = total + lax.ppermute(block[at * size : (at + 1) * size], "row", [(0, at)])
    return total


def shards(a_trail, a_panel, l_panel, a_diag, l_inverse):
    row_dev, col_dev = a_trail.shape
    nb = a_diag.shape[0]
    part = col_dev // ROWS
    row = lax.axis_index("row")
    col = lax.axis_index("col")
    raw_rows = lax.all_gather(jnp.concatenate([a_panel, l_panel], 1), "col", axis=0, tiled=True)
    a11_new = product(product(l_inverse, a_diag), l_inverse.T)
    half_term = 0.5 * product(l_panel, a11_new)
    first_y = product(a_panel, l_inverse.T) - half_term
    panel_out = first_y - half_term
    mates = gather_small(
        to_columns(jnp.concatenate([product(l_panel, l_inverse), panel_out], 1)), "row", ROWS
    )
    updated = a_trail - product3(raw_rows, mates.T)
    local = lax.iota(jnp.int32, col_dev)
    not_top = jnp.logical_or(col > 0, local >= nb)
    head = updated[: 2 * nb]
    panel_t = jnp.where(not_top[None, :], head[:nb], 0.0)
    shard = scatter_from_first_row(jnp.concatenate([panel_t, head[nb:]], 0).T)
    both_rows = lax.all_gather(to_panel(shard), "col", axis=0, tiled=True)
    panel_rows, second_rows = (both_rows[:, :nb], both_rows[:, nb:])
    corner = jnp.where(col == 0, head[nb:], 0.0)
    packed = scatter_sum(jnp.concatenate([product(panel_t, panel_t.T), corner], 1), "col", COLS)
    packed = gather_small(share(packed, "row", ROWS)[0], "col", COLS)
    gram, top_block, corner = (packed[:, :nb], packed[:, nb : 2 * nb], packed[:, 2 * nb :])
    partial = product3(updated.T, panel_rows)
    image = scatter_sum(partial, "row", ROWS)
    image_rows = lax.all_gather(to_panel(image), "col", axis=0, tiled=True)
    cols = lax.all_gather(jnp.concatenate([shard, image], 1), "row", axis=0, tiled=True)
    panel_cols, second_cols, image_cols = (cols[:, :nb], cols[:, nb : 2 * nb], cols[:, 2 * nb :])
    weights = jnp.concatenate(
        [product(shard[:, :nb].T, image), jnp.where(col == 0, partial[nb : 2 * nb], 0.0)], 1
    )
    weights = scatter_sum(weights, "col", COLS)
    weights = gather_small(jnp.sum(share(weights, "row", ROWS), axis=0), "col", COLS)
    core, image_top = (weights[:, :nb], weights[:, nb:])
    factor = jnp.linalg.cholesky(gram)
    solve = right_solve(factor, jnp.eye(nb, dtype=jnp.float32))
    g_inverse = newton_inverse_of_shifted(product(top_block, solve)).T
    image_top = product(image_top, solve)
    middle = product(product(solve.T, core), solve) + image_top + image_top.T + corner
    m_core = product(g_inverse.T, product(middle, g_inverse))
    solve_g = product(solve, g_inverse)

    def reflectors(panel, image, second, owner):
        size = panel.shape[0]
        picker = jnp.logical_and(
            lax.iota(jnp.int32, size)[:, None] - nb == lax.iota(jnp.int32, nb)[None, :], owner
        ).astype(jnp.float32)
        y_part = product3(panel, solve) + picker
        x_part = product3(image, solve_g) + product3(second, g_inverse)
        return (y_part, x_part - 0.5 * product3(y_part, m_core))

    y_rows, z_rows = reflectors(panel_rows, image_rows, second_rows, row == 0)
    y_cols, z_cols = reflectors(panel_cols, image_cols, second_cols, col == 0)
    trail_out = updated - product3(
        jnp.concatenate([z_rows, y_rows], 1), jnp.concatenate([y_cols, z_cols], 1).T
    )
    return (trail_out, panel_out)


def solution(mesh):
    return jax.shard_map(
        shards,
        mesh=mesh,
        in_specs=(P("row", "col"), P(("row", "col"), None), P(("row", "col"), None), P(), P()),
        out_specs=(P("row", "col"), P(("row", "col"), None)),
        check_vma=False,
    )
```

profile of v0, /device:TPU:1, one launch (start us, length us, event | category | flops | bytes accessed | tf_op | source)
XLA Modules:
  0.0 394.2 jit_solution(14805733286405899376)
XLA Ops:
  12.4 4.9 %collective-permute-start = (f32[64,512]{1,0:T(8,128)S(1)}, f32[64,512]{1,0:T(8,128)S(1)}, u32[]{:S(2)}, u32[]{:S(2)}) collective-permute-start(f32[64,512]{1,0:T(8,128)S(1)} %pad_maximum_fusion.3), channel_id=1, source_target_pairs={{0,0},{1,32},{2,64},{3,96},{4,128},{5,160},{6,192},{7,224},{8,1},{... | collective-permute-start | bytes 393224 | tf_op jit(solution)/shard_map/ppermute | solution.py:51
  20.7 19.2 %all-to-all-start = ((f32[8,64,512]{2,1,0:T(8,128)}), f32[8,64,512]{2,1,0:T(8,128)S(1)}, u32[]{:S(2)}, u32[]{:S(2)}) async-start(f32[8,64,512]{2,1,0:T(8,128)} %tile.12), calls=%async_computation | async-start | bytes 2097152 | tf_op jit(solution)/shard_map/all_to_all | solution.py:37
  40.0 29.2 %all-to-all-done = f32[8,64,512]{2,1,0:T(8,128)S(1)} async-done(((f32[8,64,512]{2,1,0:T(8,128)}), f32[8,64,512]{2,1,0:T(8,128)S(1)}, u32[]{:S(2)}, u32[]{:S(2)}) %all-to-all-start) | async-done | bytes 1048608 | tf_op jit(solution)/shard_map/all_to_all | solution.py:37
  69.1 8.1 %convolution_subtract_fusion = f32[2048,512]{1,0:T(8,128)S(1)} fusion(f32[2048,512]{1,0:T(8,128)} %param.5, f32[2048,512]{1,0:T(8,128)} %all-gather.5.cloned.1.call-done, f32[512,512]{1,0:T(8,128)S(1)} %bitcast.109), kind=kOutput, calls=%fused_computation.7 | convolution fusion | flops 3222274048 | bytes 13631488 | tf_op jit(solution)/shard_map/dot_general | solution.py:17
  98.9 5.5 %collective-permute-done.4 = f32[64,512]{0,1:T(8,128)} collective-permute-done((f32[64,512]{0,1:T(8,128)S(1)}, f32[64,512]{0,1:T(8,128)}, u32[]{:S(2)}, u32[]{:S(2)}) %collective-permute-start.4) | collective-permute-done | bytes 131104 | tf_op jit(solution)/shard_map/ppermute | solution.py:62
  113.3 22.2 %collective-permute-done.8 = f32[64,512]{0,1:T(8,128)S(1)} collective-permute-done((f32[64,512]{0,1:T(8,128)S(1)}, f32[64,512]{0,1:T(8,128)S(1)}, u32[]{:S(2)}, u32[]{:S(2)}) %collective-permute-start.8) | collective-permute-done | bytes 131104 | tf_op jit(solution)/shard_map/ppermute | solution.py:55
  137.0 28.0 %all_to_all.66 = f32[32,8,768]{2,1,0:T(8,128)S(1)} all-to-all(f32[32,8,768]{2,1,0:T(8,128)S(1)} %maximum_bitcast_fusion.1), channel_id=1, replica_groups=mesh['row'=8,'col'=32] {'col'}, dimensions={0} | all-to-all | bytes 1572864 | tf_op jit(solution)/shard_map/all_to_all | solution.py:46
  165.1 14.7 %all_to_all.67 = f32[8,8,768]{2,1,0:T(8,128)S(1)} all-to-all(f32[8,8,768]{2,1,0:T(8,128)S(1)} %tile.13), channel_id=1, replica_groups=mesh['row'=8,'col'=32] {'row'}, dimensions={0} | all-to-all | bytes 393216 | tf_op jit(solution)/shard_map/all_to_all | solution.py:37
  180.7 4.6 %all-to-all-start.4 = ((f32[32,8,768]{2,1,0:T(8,128)}), f32[32,8,768]{2,1,0:T(8,128)S(1)}, u32[]{:S(2)}, u32[]{:S(2)}) async-start(f32[32,8,768]{2,1,0:T(8,128)} %tile.15), calls=%async_computation.4 | async-start | bytes 1572864 | tf_op jit(solution)/shard_map/all_to_all | solution.py:37
  185.4 14.1 %all-to-all-done.4 = f32[32,8,768]{2,1,0:T(8,128)S(1)} async-done(((f32[32,8,768]{2,1,0:T(8,128)}), f32[32,8,768]{2,1,0:T(8,128)S(1)}, u32[]{:S(2)}, u32[]{:S(2)}) %all-to-all-start.4) | async-done | bytes 786464 | tf_op jit(solution)/shard_map/all_to_all | solution.py:37
  199.7 11.7 %cholesky.50 = f32[128,128]{1,0:T(8,128)S(1)} custom-call(f32[128,128]{1,0:T(8,128)S(1)} %cholesky.118), custom_call_target="Cholesky" | custom-call | tf_op jit(solution)/shard_map/jit(cholesky)/cholesky | solution.py:103
  211.5 9.8 %custom-call.14 = f32[1,128,128]{1,2,0:T(8,128)S(1)} custom-call(f32[1,128,128]{2,1,0:T(8,128)S(1)} %get-tuple-element.33), custom_call_target="InvertDiagBlocksLowerTriangular" | custom-call | tf_op jit(solution)/shard_map/jit(cholesky)/cholesky | solution.py:103
  221.8 11.7 %cholesky.105 = f32[128,128]{1,0:T(8,128)S(1)} custom-call(f32[128,128]{1,0:T(8,128)S(1)} %convolution_subtract_fusion.2), custom_call_target="Cholesky" | custom-call | tf_op jit(solution)/shard_map/jit(cholesky)/cholesky | solution.py:103
  239.3 19.8 %custom-call.15 = f32[2,128,128]{1,2,0:T(8,128)S(1)} custom-call(f32[2,128,128]{2,1,0:T(8,128)S(1)} %get-tuple-element.9), custom_call_target="InvertDiagBlocksLowerTriangular" | custom-call | tf_op jit(solution)/shard_map/triangular_solve | solution.py:21
  259.9 7.1 %fusion.12 = f32[512,256]{1,0:T(8,128)} fusion(f32[2048,512]{1,0:T(8,128)} %copy-done.1, f32[2048,512]{1,0:T(8,128)} %all-gather.7.cloned.1.call-done), kind=kOutput, calls=%fused_computation.17 | convolution fusion | flops 1610612736 | bytes 6815744 | tf_op jit(solution)/shard_map/dot_general | solution.py:17
  267.0 5.2 %all-to-all-start.1 = ((f32[8,64,256]{2,1,0:T(8,128)}), f32[8,64,256]{2,1,0:T(8,128)S(1)}, u32[]{:S(2)}, u32[]{:S(2)}) async-start(f32[8,64,256]{2,1,0:T(8,128)} %bitcast.3), calls=%async_computation.1 | async-start | bytes 1048576 | tf_op jit(solution)/shard_map/all_to_all | solution.py:46
  273.8 16.4 %all-to-all-done.1 = f32[8,64,256]{2,1,0:T(8,128)S(1)} async-done(((f32[8,64,256]{2,1,0:T(8,128)}), f32[8,64,256]{2,1,0:T(8,128)S(1)}, u32[]{:S(2)}, u32[]{:S(2)}) %all-to-all-start.1) | async-done | bytes 524320 | tf_op jit(solution)/shard_map/all_to_all | solution.py:46
  299.5 7.1 %all-to-all-start.5 = ((f32[32,8,512]{2,1,0:T(8,128)}), f32[32,8,512]{2,1,0:T(8,128)S(1)}, u32[]{:S(2)}, u32[]{:S(2)}) async-start(f32[32,8,512]{2,1,0:T(8,128)} %maximum_bitcast_fusion.2), calls=%async_computation.5 | async-start | bytes 1048576 | tf_op jit(solution)/shard_map/all_to_all | solution.py:46
  308.7 9.5 %all-to-all-done.5 = f32[32,8,512]{2,1,0:T(8,128)S(1)} async-done(((f32[32,8,512]{2,1,0:T(8,128)}), f32[32,8,512]{2,1,0:T(8,128)S(1)}, u32[]{:S(2)}, u32[]{:S(2)}) %all-to-all-start.5) | async-done | bytes 524320 | tf_op jit(solution)/shard_map/all_to_all | solution.py:46
  319.0 4.9 %all-to-all-start.6 = ((f32[8,8,512]{2,1,0:T(8,128)}), f32[8,8,512]{2,1,0:T(8,128)S(1)}, u32[]{:S(2)}, u32[]{:S(2)}) async-start(f32[8,8,512]{2,1,0:T(8,128)} %tile.16), calls=%async_computation.6 | async-start | bytes 262144 | tf_op jit(solution)/shard_map/all_to_all | solution.py:37
  325.1 8.0 %all-to-all-done.6 = f32[8,8,512]{2,1,0:T(8,128)S(1)} async-done(((f32[8,8,512]{2,1,0:T(8,128)}), f32[8,8,512]{2,1,0:T(8,128)S(1)}, u32[]{:S(2)}, u32[]{:S(2)}) %all-to-all-start.6) | async-done | bytes 131104 | tf_op jit(solution)/shard_map/all_to_all | solution.py:37
  343.7 6.7 %all-to-all-done.7 = f32[32,8,512]{2,1,0:T(8,128)S(1)} async-done(((f32[32,8,512]{2,1,0:T(8,128)}), f32[32,8,512]{2,1,0:T(8,128)S(1)}, u32[]{:S(2)}, u32[]{:S(2)}) %all-to-all-start.7) | async-done | bytes 524320 | tf_op jit(solution)/shard_map/all_to_all | solution.py:37
  365.2 12.7 %all-gather.9.cloned.1.call-done = f32[2048,256]{1,0:T(8,128)} async-done(((f32[64,256]{1,0:T(8,128)}), f32[2048,256]{1,0:T(8,128)}) %all-gather.9.cloned.1.call-update) | async-done | bytes 2097168 | tf_op jit(solution)/shard_map/all_gather | solution.py:94
  382.2 5.2 %fusion.4 = f32[2048,512]{1,0:T(8,128)} fusion(f32[2048,512]{1,0:T(8,128)S(1)} %copy-done.2, f32[2048,256]{0,1:T(8,128)S(1)} %convolution_add_fusion, f32[2048,256]{0,1:T(8,128)S(1)} %fusion.7, f32[512,256]{0,1:T(8,128)S(1)} %copy-done.9, f32[512,256]{0,1:T(8,128)S(1)} %convolution_add_fusion.3), kind=kOutput, calls=%fused_computation.6 | convolution fusion | flops 3223584768 | bytes 13631488 | tf_op jit(solution)/shard_map/dot_general | solution.py:17
  (150 shorter events, 95.5 us)
Async XLA Ops:
  7.2 4.8 %copy-start.13 = (f32[64,256]{1,0:T(8,128)S(1)}, f32[64,256]{1,0:T(8,128)}, u32[]{:S(2)}) copy-start(f32[64,256]{1,0:T(8,128)} %param.6) | copy-start | bytes 196612
  7.2 61.9 %all-gather.5.cloned.1.call-start = ((), (), s32[]{:S(2)}) async-start(), calls=%async_computation.8 | async-start | bytes 4325376 | tf_op jit(solution)/shard_map/all_gather | solution.py:72
  12.4 64.9 %copy-start.14 = (f32[64,256]{1,0:T(8,128)}, f32[64,256]{1,0:T(8,128)S(1)}, u32[]{:S(2)}) copy-start(f32[64,256]{1,0:T(8,128)S(1)} %fusion.18) | copy-start | bytes 196612
  12.4 7.2 %collective-permute-start = (f32[64,512]{1,0:T(8,128)S(1)}, f32[64,512]{1,0:T(8,128)S(1)}, u32[]{:S(2)}, u32[]{:S(2)}) collective-permute-start(f32[64,512]{1,0:T(8,128)S(1)} %pad_maximum_fusion.3), channel_id=1, source_target_pairs={{0,0},{1,32},{2,64},{3,96},{4,128},{5,160},{6,192},{7,224},{8,1},{... | collective-permute-start | bytes 393224 | tf_op jit(solution)/shard_map/ppermute | solution.py:51
  20.7 48.5 %all-to-all-start = ((f32[8,64,512]{2,1,0:T(8,128)}), f32[8,64,512]{2,1,0:T(8,128)S(1)}, u32[]{:S(2)}, u32[]{:S(2)}) async-start(f32[8,64,512]{2,1,0:T(8,128)} %tile.12), calls=%async_computation | async-start | bytes 2097152 | tf_op jit(solution)/shard_map/all_to_all | solution.py:37
  39.9 219.9 %all-gather.7.cloned.1.call-start = ((), (), s32[]{:S(2)}) async-start(), calls=%async_computation.9 | async-start | bytes 4325376 | tf_op jit(solution)/shard_map/all_gather | solution.py:86
  80.3 11.7 %collective-permute-start.1 = (f32[64,512]{0,1:T(8,128)S(1)}, f32[64,512]{0,1:T(8,128)S(1)}, u32[]{:S(2)}, u32[]{:S(2)}) collective-permute-start(f32[64,512]{0,1:T(8,128)S(1)} %get-tuple-element.23), channel_id=1, source_target_pairs={{0,32},{1,33},{2,34},{3,35},{4,36},{5,37},{6,38},{7,39},{8,40},{9,... | collective-permute-start | bytes 393224 | tf_op jit(solution)/shard_map/ppermute | solution.py:62
  82.5 11.6 %collective-permute-start.2 = (f32[64,512]{0,1:T(8,128)S(1)}, f32[64,512]{0,1:T(8,128)S(1)}, u32[]{:S(2)}, u32[]{:S(2)}) collective-permute-start(f32[64,512]{0,1:T(8,128)S(1)} %get-tuple-element.29), channel_id=1, source_target_pairs={{0,64},{1,65},{2,66},{3,67},{4,68},{5,69},{6,70},{7,71},{8,72},{9,... | collective-permute-start | bytes 393224 | tf_op jit(solution)/shard_map/ppermute | solution.py:62
  84.1 14.8 %collective-permute-start.3 = (f32[64,512]{0,1:T(8,128)}, f32[64,512]{0,1:T(8,128)}, u32[]{:S(2)}, u32[]{:S(2)}) collective-permute-start(f32[64,512]{0,1:T(8,128)} %get-tuple-element.28), channel_id=1, source_target_pairs={{0,96},{1,97},{2,98},{3,99},{4,100},{5,101},{6,102},{7,103},{8,104... | collective-permute-start | bytes 393224 | tf_op jit(solution)/shard_map/ppermute | solution.py:62
  86.5 17.9 %collective-permute-start.4 = (f32[64,512]{0,1:T(8,128)S(1)}, f32[64,512]{0,1:T(8,128)}, u32[]{:S(2)}, u32[]{:S(2)}) collective-permute-start(f32[64,512]{0,1:T(8,128)S(1)} %get-tuple-element.27), channel_id=1, source_target_pairs={{0,128},{1,129},{2,130},{3,131},{4,132},{5,133},{6,134},{7,135},{8... | collective-permute-start | bytes 393224 | tf_op jit(solution)/shard_map/ppermute | solution.py:62
  90.0 14.4 %collective-permute-start.5 = (f32[64,512]{0,1:T(8,128)S(1)}, f32[64,512]{0,1:T(8,128)}, u32[]{:S(2)}, u32[]{:S(2)}) collective-permute-start(f32[64,512]{0,1:T(8,128)S(1)} %get-tuple-element.26), channel_id=1, source_target_pairs={{0,160},{1,161},{2,162},{3,163},{4,164},{5,165},{6,166},{7,167},{8... | collective-permute-start | bytes 393224 | tf_op jit(solution)/shard_map/ppermute | solution.py:62
  92.0 12.4 %collective-permute-start.6 = (f32[64,512]{0,1:T(8,128)S(1)}, f32[64,512]{0,1:T(8,128)}, u32[]{:S(2)}, u32[]{:S(2)}) collective-permute-start(f32[64,512]{0,1:T(8,128)S(1)} %get-tuple-element.25), channel_id=1, source_target_pairs={{0,192},{1,193},{2,194},{3,195},{4,196},{5,197},{6,198},{7,199},{8... | collective-permute-start | bytes 393224 | tf_op jit(solution)/shard_map/ppermute | solution.py:62
  94.8 13.2 %collective-permute-start.7 = (f32[64,512]{0,1:T(8,128)S(1)}, f32[64,512]{0,1:T(8,128)}, u32[]{:S(2)}, u32[]{:S(2)}) collective-permute-start(f32[64,512]{0,1:T(8,128)S(1)} %get-tuple-element.24), channel_id=1, source_target_pairs={{0,224},{1,225},{2,226},{3,227},{4,228},{5,229},{6,230},{7,231},{8... | collective-permute-start | bytes 393224 | tf_op jit(solution)/shard_map/ppermute | solution.py:62
  109.5 26.0 %collective-permute-start.8 = (f32[64,512]{0,1:T(8,128)S(1)}, f32[64,512]{0,1:T(8,128)S(1)}, u32[]{:S(2)}, u32[]{:S(2)}) collective-permute-start(f32[64,512]{0,1:T(8,128)S(1)} %fusion.38), channel_id=1, source_target_pairs={{0,0},{32,1},{64,2},{96,3},{128,4},{160,5},{192,6},{224,7},{1,8},{... | collective-permute-start | bytes 393224 | tf_op jit(solution)/shard_map/ppermute | solution.py:55
  180.7 18.8 %all-to-all-start.4 = ((f32[32,8,768]{2,1,0:T(8,128)}), f32[32,8,768]{2,1,0:T(8,128)S(1)}, u32[]{:S(2)}, u32[]{:S(2)}) async-start(f32[32,8,768]{2,1,0:T(8,128)} %tile.15), calls=%async_computation.4 | async-start | bytes 1572864 | tf_op jit(solution)/shard_map/all_to_all | solution.py:37
  199.5 73.1 %copy-start.4 = (f32[32,8,768]{2,1,0:T(8,128)}, f32[32,8,768]{2,1,0:T(8,128)S(1)}, u32[]{:S(2)}) copy-start(f32[32,8,768]{2,1,0:T(8,128)S(1)} %all-to-all-done.4) | copy-start | bytes 2359300
  267.0 23.2 %all-to-all-start.1 = ((f32[8,64,256]{2,1,0:T(8,128)}), f32[8,64,256]{2,1,0:T(8,128)S(1)}, u32[]{:S(2)}, u32[]{:S(2)}) async-start(f32[8,64,256]{2,1,0:T(8,128)} %bitcast.3), calls=%async_computation.1 | async-start | bytes 1048576 | tf_op jit(solution)/shard_map/all_to_all | solution.py:46
  272.2 87.2 %all-gather.11.cloned.1.call-start = ((), (), s32[]{:S(2)}) async-start(), calls=%async_computation.11 | async-start | bytes 1769472 | tf_op jit(solution)/shard_map/all_gather | solution.py:95
  295.6 11.3 %collective-permute-start.9 = (f32[64,256]{1,0:T(8,128)S(1)}, f32[64,256]{1,0:T(8,128)S(1)}, u32[]{:S(2)}, u32[]{:S(2)}) collective-permute-start(f32[64,256]{1,0:T(8,128)S(1)} %reduce_sum.36), channel_id=1, source_target_pairs={{0,0},{32,1},{64,2},{96,3},{128,4},{160,5},{192,6},{224,7},{1,8},{... | collective-permute-start | bytes 196616 | tf_op jit(solution)/shard_map/ppermute | solution.py:55
  299.5 18.8 %all-to-all-start.5 = ((f32[32,8,512]{2,1,0:T(8,128)}), f32[32,8,512]{2,1,0:T(8,128)S(1)}, u32[]{:S(2)}, u32[]{:S(2)}) async-start(f32[32,8,512]{2,1,0:T(8,128)} %maximum_bitcast_fusion.2), calls=%async_computation.5 | async-start | bytes 1048576 | tf_op jit(solution)/shard_map/all_to_all | solution.py:46
  306.7 71.3 %all-gather.9.cloned.1.call-start = ((), (), s32[]{:S(2)}) async-start(), calls=%async_computation.10 | async-start | bytes 2162688 | tf_op jit(solution)/shard_map/all_gather | solution.py:94
  319.0 14.1 %all-to-all-start.6 = ((f32[8,8,512]{2,1,0:T(8,128)}), f32[8,8,512]{2,1,0:T(8,128)S(1)}, u32[]{:S(2)}, u32[]{:S(2)}) async-start(f32[8,8,512]{2,1,0:T(8,128)} %tile.16), calls=%async_computation.6 | async-start | bytes 262144 | tf_op jit(solution)/shard_map/all_to_all | solution.py:37
  334.0 16.4 %all-to-all-start.7 = ((f32[32,8,512]{2,1,0:T(8,128)}), f32[32,8,512]{2,1,0:T(8,128)S(1)}, u32[]{:S(2)}, u32[]{:S(2)}) async-start(f32[32,8,512]{2,1,0:T(8,128)} %tile.17), calls=%async_computation.7 | async-start | bytes 1048576 | tf_op jit(solution)/shard_map/all_to_all | solution.py:37
  362.5 15.5 %copy-start.5 = (f32[256,256]{1,0:T(8,128)S(1)}, f32[256,256]{1,0:T(8,128)}, u32[]{:S(2)}) copy-start(f32[256,256]{1,0:T(8,128)} %fusion.54) | copy-start | bytes 786436
  (12 other events, 29.2 us)
Sparse Core Ops, SparseCore 0:
  10.6 57.4 all-gather.4
  136.4 56.2 all-gather.6
  291.3 32.7 all-gather.10
  326.5 51.3 all-gather.8
where the time goes:
time: 401 us; the launch traced here: 394 us
  waiting for transfers between devices  132 us (33%)
  starting transfers between devices  72.6 us (18%)
  other arithmetic  59.5 us (15%)
  matrix products  56.1 us (14%)
  blocking collectives  42.7 us (11%)
  between operations  15.9 us (4%)
  local copies, waits for them, and re-layouts  15 us (4%)
    all_to_all x4, waiting for transfers between devices, share(): parts = lax.all_to_all(jnp.tile(block, (size, 1)), axis, 0, 0, tiled=True)  58 us
    dot_general x11, matrix products, product3(): jnp.dot(left, right, precision=lax.Precision.HIGH, preferred_element_type...  38.3 us
    another operation x6, other arithmetic, shards(): factor = jnp.linalg.cholesky(gram)  34 us
    all_to_all x4, starting transfers between devices, share(): parts = lax.all_to_all(jnp.tile(block, (size, 1)), axis, 0, 0, tiled=True)  32.9 us
    all_to_all x1, blocking collectives, scatter_sum(): parts = lax.all_to_all(block, axis, 0, 0, tiled=True)  28 us
    all_to_all x2, waiting for transfers between devices, scatter_sum(): parts = lax.all_to_all(block, axis, 0, 0, tiled=True)  25.9 us
    ppermute x2, waiting for transfers between devices, to_panel(): lax.ppermute(block, BOTH, [(at % 8 * COLS + at // 8, at) for at in range(...  22.2 us
    another operation x3, other arithmetic, right_solve(): lax.linalg.triangular_solve(factor, values, left_side=False, lower=True,...  19.9 us
  transfers between devices with their start and end apart: 20, of which 12 were waited for; matrix products, arithmetic and copies ran while one was open for 24% of the time, Pallas kernels for 0%

commit v1 on v0

--- a/solution.py
+++ b/solution.py
@@ -91,7 +91,9 @@
     gram, top_block, corner = (packed[:, :nb], packed[:, nb : 2 * nb], packed[:, 2 * nb :])
     partial = product3(updated.T, panel_rows)
     image = scatter_sum(partial, "row", ROWS)
-    image_rows = lax.all_gather(to_panel(image), "col", axis=0, tiled=True)
+    image_rows = jnp.concatenate(
+        lax.all_to_all(jnp.stack([to_panel(image)] * lax.axis_size("col")), "col", 0, 0), axis=0
+    )
     cols = lax.all_gather(jnp.concatenate([shard, image], 1), "row", axis=0, tiled=True)
     panel_cols, second_cols, image_cols = (cols[:, :nb], cols[:, nb : 2 * nb], cols[:, 2 * nb :])
     weights = jnp.concatenate(

time: 401 us -> 414 us (1.032)
  starting transfers between devices: 72.6 us -> 81.1 us
  waiting for transfers between devices: 132 us -> 139 us
    all_to_all x0 -> x1, waiting for transfers between devices: none -> 15.7 us  [shards(): lax.all_to_all(jnp.stack([to_panel(image)] * lax.axis_size('col')), 'col'...]
    all_gather x1 -> x0, waiting for transfers between devices: 12.7 us -> none  [shards(): image_rows = lax.all_gather(to_panel(image), 'col', axis=0, tiled=True)]
    all_to_all x0 -> x1, starting transfers between devices: none -> 11.9 us  [shards(): lax.all_to_all(jnp.stack([to_panel(image)] * lax.axis_size('col')), 'col'...]
  transfers between devices with their start and end apart: 20 -> 20, of which waited for: 12 -> 14; matrix products, arithmetic and copies ran while one was open for 24% -> 23% of each run, Pallas kernels for 0% -> 0%
where the time goes in v1:
time: 414 us; the launch traced here: 407 us
  waiting for transfers between devices  139 us (34%)
  starting transfers between devices  81.1 us (20%)
  other arithmetic  59.4 us (14%)
  matrix products  54.9 us (13%)
  blocking collectives  41.4 us (10%)
  between operations  15.8 us (4%)
  local copies, waits for them, and re-layouts  15.1 us (4%)
    all_to_all x4, waiting for transfers between devices, share(): parts = lax.all_to_all(jnp.tile(block, (size, 1)), axis, 0, 0, tiled=True)  56.3 us
    dot_general x11, matrix products, product3(): jnp.dot(left, right, precision=lax.Precision.HIGH, preferred_element_type...  38.7 us
    another operation x6, other arithmetic, shards(): factor = jnp.linalg.cholesky(gram)  33.9 us
    all_to_all x4, starting transfers between devices, share(): parts = lax.all_to_all(jnp.tile(block, (size, 1)), axis, 0, 0, tiled=True)  31.3 us
    all_to_all x1, blocking collectives, scatter_sum(): parts = lax.all_to_all(block, axis, 0, 0, tiled=True)  27.2 us
    all_to_all x2, waiting for transfers between devices, scatter_sum(): parts = lax.all_to_all(block, axis, 0, 0, tiled=True)  26.3 us
    ppermute x2, waiting for transfers between devices, to_panel(): lax.ppermute(block, BOTH, [(at % 8 * COLS + at // 8, at) for at in range(...  24 us
    another operation x3, other arithmetic, right_solve(): lax.linalg.triangular_solve(factor, values, left_side=False, lower=True,...  19.9 us
  transfers between devices with their start and end apart: 20, of which 14 were waited for; matrix products, arithmetic and copies ran while one was open for 23% of the time, Pallas kernels for 0%

profile of v1, /device:TPU:1, one launch (start us, length us, event | category | flops | bytes accessed | tf_op | source)
XLA Modules:
  0.0 407.1 jit_solution(16712418254815661263)
XLA Ops:
  12.4 4.9 %collective-permute-start = (f32[64,512]{1,0:T(8,128)S(1)}, f32[64,512]{1,0:T(8,128)S(1)}, u32[]{:S(2)}, u32[]{:S(2)}) collective-permute-start(f32[64,512]{1,0:T(8,128)S(1)} %pad_maximum_fusion.3), channel_id=1, source_target_pairs={{0,0},{1,32},{2,64},{3,96},{4,128},{5,160},{6,192},{7,224},{8,1},{... | collective-permute-start | bytes 393224 | tf_op jit(solution)/shard_map/ppermute | solution.py:51
  20.7 19.2 %all-to-all-start = ((f32[8,64,512]{2,1,0:T(8,128)}), f32[8,64,512]{2,1,0:T(8,128)S(1)}, u32[]{:S(2)}, u32[]{:S(2)}) async-start(f32[8,64,512]{2,1,0:T(8,128)} %tile.12), calls=%async_computation | async-start | bytes 2097152 | tf_op jit(solution)/shard_map/all_to_all | solution.py:37
  40.0 29.2 %all-to-all-done = f32[8,64,512]{2,1,0:T(8,128)S(1)} async-done(((f32[8,64,512]{2,1,0:T(8,128)}), f32[8,64,512]{2,1,0:T(8,128)S(1)}, u32[]{:S(2)}, u32[]{:S(2)}) %all-to-all-start) | async-done | bytes 1048608 | tf_op jit(solution)/shard_map/all_to_all | solution.py:37
  69.2 8.1 %convolution_subtract_fusion = f32[2048,512]{1,0:T(8,128)S(1)} fusion(f32[2048,512]{1,0:T(8,128)} %param.5, f32[2048,512]{1,0:T(8,128)} %all-gather.4.cloned.1.call-done, f32[512,512]{1,0:T(8,128)S(1)} %bitcast.110), kind=kOutput, calls=%fused_computation.7 | convolution fusion | flops 3222274048 | bytes 13631488 | tf_op jit(solution)/shard_map/dot_general | solution.py:17
  101.1 5.0 %collective-permute-done.2 = f32[64,512]{0,1:T(8,128)} collective-permute-done((f32[64,512]{0,1:T(8,128)S(1)}, f32[64,512]{0,1:T(8,128)}, u32[]{:S(2)}, u32[]{:S(2)}) %collective-permute-start.2) | collective-permute-done | bytes 131104 | tf_op jit(solution)/shard_map/ppermute | solution.py:62
  106.1 5.6 %collective-permute-done.1 = f32[64,512]{0,1:T(8,128)} collective-permute-done((f32[64,512]{0,1:T(8,128)S(1)}, f32[64,512]{0,1:T(8,128)}, u32[]{:S(2)}, u32[]{:S(2)}) %collective-permute-start.1) | collective-permute-done | bytes 131104 | tf_op jit(solution)/shard_map/ppermute | solution.py:62
  117.0 21.8 %collective-permute-done.8 = f32[64,512]{0,1:T(8,128)S(1)} collective-permute-done((f32[64,512]{0,1:T(8,128)S(1)}, f32[64,512]{0,1:T(8,128)S(1)}, u32[]{:S(2)}, u32[]{:S(2)}) %collective-permute-start.8) | collective-permute-done | bytes 131104 | tf_op jit(solution)/shard_map/ppermute | solution.py:55
  140.3 27.2 %all_to_all.71 = f32[32,8,768]{2,1,0:T(8,128)S(1)} all-to-all(f32[32,8,768]{2,1,0:T(8,128)S(1)} %maximum_bitcast_fusion.1), channel_id=1, replica_groups=mesh['row'=8,'col'=32] {'col'}, dimensions={0} | all-to-all | bytes 1572864 | tf_op jit(solution)/shard_map/all_to_all | solution.py:46
  167.6 14.2 %all_to_all.72 = f32[8,8,768]{2,1,0:T(8,128)S(1)} all-to-all(f32[8,8,768]{2,1,0:T(8,128)S(1)} %tile.13), channel_id=1, replica_groups=mesh['row'=8,'col'=32] {'row'}, dimensions={0} | all-to-all | bytes 393216 | tf_op jit(solution)/shard_map/all_to_all | solution.py:37
  187.4 14.1 %all-to-all-done.5 = f32[32,8,768]{2,1,0:T(8,128)S(1)} async-done(((f32[32,8,768]{2,1,0:T(8,128)}), f32[32,8,768]{2,1,0:T(8,128)S(1)}, u32[]{:S(2)}, u32[]{:S(2)}) %all-to-all-start.5) | async-done | bytes 786464 | tf_op jit(solution)/shard_map/all_to_all | solution.py:37
  201.7 11.7 %cholesky.50 = f32[128,128]{1,0:T(8,128)S(1)} custom-call(f32[128,128]{1,0:T(8,128)S(1)} %cholesky.118), custom_call_target="Cholesky" | custom-call | tf_op jit(solution)/shard_map/jit(cholesky)/cholesky | solution.py:105
  213.5 9.8 %custom-call.14 = f32[1,128,128]{1,2,0:T(8,128)S(1)} custom-call(f32[1,128,128]{2,1,0:T(8,128)S(1)} %get-tuple-element.33), custom_call_target="InvertDiagBlocksLowerTriangular" | custom-call | tf_op jit(solution)/shard_map/jit(cholesky)/cholesky | solution.py:105
  223.8 11.7 %cholesky.105 = f32[128,128]{1,0:T(8,128)S(1)} custom-call(f32[128,128]{1,0:T(8,128)S(1)} %convolution_subtract_fusion.2), custom_call_target="Cholesky" | custom-call | tf_op jit(solution)/shard_map/jit(cholesky)/cholesky | solution.py:105
  241.0 19.8 %custom-call.15 = f32[2,128,128]{1,2,0:T(8,128)S(1)} custom-call(f32[2,128,128]{2,1,0:T(8,128)S(1)} %get-tuple-element.9), custom_call_target="InvertDiagBlocksLowerTriangular" | custom-call | tf_op jit(solution)/shard_map/triangular_solve | solution.py:21
  264.6 7.1 %fusion.12 = f32[512,256]{1,0:T(8,128)} fusion(f32[2048,512]{1,0:T(8,128)} %copy-done.1, f32[2048,512]{1,0:T(8,128)} %all-gather.6.cloned.1.call-done), kind=kOutput, calls=%fused_computation.17 | convolution fusion | flops 1610612736 | bytes 6815744 | tf_op jit(solution)/shard_map/dot_general | solution.py:17
  271.8 4.7 %all-to-all-start.1 = ((f32[8,64,256]{2,1,0:T(8,128)}), f32[8,64,256]{2,1,0:T(8,128)S(1)}, u32[]{:S(2)}, u32[]{:S(2)}) async-start(f32[8,64,256]{2,1,0:T(8,128)} %bitcast.3), calls=%async_computation.1 | async-start | bytes 1048576 | tf_op jit(solution)/shard_map/all_to_all | solution.py:46
  278.6 15.8 %all-to-all-done.1 = f32[8,64,256]{2,1,0:T(8,128)S(1)} async-done(((f32[8,64,256]{2,1,0:T(8,128)}), f32[8,64,256]{2,1,0:T(8,128)S(1)}, u32[]{:S(2)}, u32[]{:S(2)}) %all-to-all-start.1) | async-done | bytes 524320 | tf_op jit(solution)/shard_map/all_to_all | solution.py:46
  295.7 5.0 %all-to-all-start.6 = ((f32[32,8,512]{2,1,0:T(8,128)}), f32[32,8,512]{2,1,0:T(8,128)S(1)}, u32[]{:S(2)}, u32[]{:S(2)}) async-start(f32[32,8,512]{2,1,0:T(8,128)} %maximum_bitcast_fusion.2), calls=%async_computation.6 | async-start | bytes 1048576 | tf_op jit(solution)/shard_map/all_to_all | solution.py:46
  301.9 10.5 %all-to-all-done.6 = f32[32,8,512]{2,1,0:T(8,128)S(1)} async-done(((f32[32,8,512]{2,1,0:T(8,128)}), f32[32,8,512]{2,1,0:T(8,128)S(1)}, u32[]{:S(2)}, u32[]{:S(2)}) %all-to-all-start.6) | async-done | bytes 524320 | tf_op jit(solution)/shard_map/all_to_all | solution.py:46
  317.1 9.1 %all-to-all-done.7 = f32[8,8,512]{2,1,0:T(8,128)S(1)} async-done(((f32[8,8,512]{2,1,0:T(8,128)}), f32[8,8,512]{2,1,0:T(8,128)S(1)}, u32[]{:S(2)}, u32[]{:S(2)}) %all-to-all-start.7) | async-done | bytes 131104 | tf_op jit(solution)/shard_map/all_to_all | solution.py:37
  344.4 11.9 %all-to-all-start.2 = ((f32[32,64,256]{2,1,0:T(8,128)}), f32[32,64,256]{2,1,0:T(8,128)}, u32[]{:S(2)}, u32[]{:S(2)}) async-start(f32[32,64,256]{2,1,0:T(8,128)} %stack.2), calls=%async_computation.2 | async-start | bytes 4194304 | tf_op jit(solution)/shard_map/all_to_all | solution.py:95
  368.9 15.7 %all-to-all-done.2 = f32[32,64,256]{2,1,0:T(8,128)} async-done(((f32[32,64,256]{2,1,0:T(8,128)}), f32[32,64,256]{2,1,0:T(8,128)}, u32[]{:S(2)}, u32[]{:S(2)}) %all-to-all-start.2) | async-done | bytes 2097184 | tf_op jit(solution)/shard_map/all_to_all | solution.py:95
  384.6 5.3 %fusion.7 = f32[2048,256]{0,1:T(8,128)} fusion(f32[2048,256]{0,1:T(8,128)} %convolution_multiply_fusion, f32[2048,256]{0,1:T(8,128)} %fusion.8, f32[2048,256]{1,0:T(8,128)} %bitcast.4, f32[256,256]{1,0:T(8,128)S(1)} %fusion.54), kind=kOutput, calls=%fused_computation.11 | convolution fusion | flops 806354944 | bytes 8650752 | tf_op jit(solution)/shard_map/dot_general | solution.py:17
  395.1 5.2 %fusion.4 = f32[2048,512]{1,0:T(8,128)} fusion(f32[2048,512]{1,0:T(8,128)S(1)} %copy-done.2, f32[2048,256]{0,1:T(8,128)S(1)} %convolution_add_fusion, f32[2048,256]{0,1:T(8,128)S(1)} %copy-done.4, f32[512,256]{0,1:T(8,128)S(1)} %fusion.14, f32[512,256]{0,1:T(8,128)S(1)} %convolution_add_fusion.3), kind=kOutput, calls=%fused_computation.6 | convolution fusion | flops 3223584768 | bytes 13631488 | tf_op jit(solution)/shard_map/dot_general | solution.py:17
  (144 shorter events, 102.1 us)
Async XLA Ops:
  7.2 4.8 %copy-start.11 = (f32[64,256]{1,0:T(8,128)S(1)}, f32[64,256]{1,0:T(8,128)}, u32[]{:S(2)}) copy-start(f32[64,256]{1,0:T(8,128)} %param.6) | copy-start | bytes 196612
  7.2 62.0 %all-gather.4.cloned.1.call-start = ((), (), s32[]{:S(2)}) async-start(), calls=%async_computation.9 | async-start | bytes 4325376 | tf_op jit(solution)/shard_map/all_gather | solution.py:72
  12.4 64.9 %copy-start.12 = (f32[64,256]{1,0:T(8,128)}, f32[64,256]{1,0:T(8,128)S(1)}, u32[]{:S(2)}) copy-start(f32[64,256]{1,0:T(8,128)S(1)} %fusion.18) | copy-start | bytes 196612
  12.4 7.2 %collective-permute-start = (f32[64,512]{1,0:T(8,128)S(1)}, f32[64,512]{1,0:T(8,128)S(1)}, u32[]{:S(2)}, u32[]{:S(2)}) collective-permute-start(f32[64,512]{1,0:T(8,128)S(1)} %pad_maximum_fusion.3), channel_id=1, source_target_pairs={{0,0},{1,32},{2,64},{3,96},{4,128},{5,160},{6,192},{7,224},{8,1},{... | collective-permute-start | bytes 393224 | tf_op jit(solution)/shard_map/ppermute | solution.py:51
  20.7 48.5 %all-to-all-start = ((f32[8,64,512]{2,1,0:T(8,128)}), f32[8,64,512]{2,1,0:T(8,128)S(1)}, u32[]{:S(2)}, u32[]{:S(2)}) async-start(f32[8,64,512]{2,1,0:T(8,128)} %tile.12), calls=%async_computation | async-start | bytes 2097152 | tf_op jit(solution)/shard_map/all_to_all | solution.py:37
  39.9 224.7 %all-gather.6.cloned.1.call-start = ((), (), s32[]{:S(2)}) async-start(), calls=%async_computation.10 | async-start | bytes 4325376 | tf_op jit(solution)/shard_map/all_gather | solution.py:86
  80.4 11.8 %collective-permute-start.7 = (f32[64,512]{0,1:T(8,128)S(1)}, f32[64,512]{0,1:T(8,128)S(1)}, u32[]{:S(2)}, u32[]{:S(2)}) collective-permute-start(f32[64,512]{0,1:T(8,128)S(1)} %get-tuple-element.24), channel_id=1, source_target_pairs={{0,224},{1,225},{2,226},{3,227},{4,228},{5,229},{6,230},{7,231},{8... | collective-permute-start | bytes 393224 | tf_op jit(solution)/shard_map/ppermute | solution.py:62
  84.3 11.0 %collective-permute-start.6 = (f32[64,512]{0,1:T(8,128)S(1)}, f32[64,512]{0,1:T(8,128)S(1)}, u32[]{:S(2)}, u32[]{:S(2)}) collective-permute-start(f32[64,512]{0,1:T(8,128)S(1)} %get-tuple-element.25), channel_id=1, source_target_pairs={{0,192},{1,193},{2,194},{3,195},{4,196},{5,197},{6,198},{7,199},{8... | collective-permute-start | bytes 393224 | tf_op jit(solution)/shard_map/ppermute | solution.py:62
  85.8 15.3 %collective-permute-start.5 = (f32[64,512]{0,1:T(8,128)}, f32[64,512]{0,1:T(8,128)}, u32[]{:S(2)}, u32[]{:S(2)}) collective-permute-start(f32[64,512]{0,1:T(8,128)} %get-tuple-element.26), channel_id=1, source_target_pairs={{0,160},{1,161},{2,162},{3,163},{4,164},{5,165},{6,166},{7,167},{8... | collective-permute-start | bytes 393224 | tf_op jit(solution)/shard_map/ppermute | solution.py:62
  88.0 13.1 %collective-permute-start.4 = (f32[64,512]{0,1:T(8,128)S(1)}, f32[64,512]{0,1:T(8,128)}, u32[]{:S(2)}, u32[]{:S(2)}) collective-permute-start(f32[64,512]{0,1:T(8,128)S(1)} %get-tuple-element.27), channel_id=1, source_target_pairs={{0,128},{1,129},{2,130},{3,131},{4,132},{5,133},{6,134},{7,135},{8... | collective-permute-start | bytes 393224 | tf_op jit(solution)/shard_map/ppermute | solution.py:62
  90.2 10.9 %collective-permute-start.3 = (f32[64,512]{0,1:T(8,128)S(1)}, f32[64,512]{0,1:T(8,128)}, u32[]{:S(2)}, u32[]{:S(2)}) collective-permute-start(f32[64,512]{0,1:T(8,128)S(1)} %get-tuple-element.28), channel_id=1, source_target_pairs={{0,96},{1,97},{2,98},{3,99},{4,100},{5,101},{6,102},{7,103},{8,104... | collective-permute-start | bytes 393224 | tf_op jit(solution)/shard_map/ppermute | solution.py:62
  92.2 13.9 %collective-permute-start.2 = (f32[64,512]{0,1:T(8,128)S(1)}, f32[64,512]{0,1:T(8,128)}, u32[]{:S(2)}, u32[]{:S(2)}) collective-permute-start(f32[64,512]{0,1:T(8,128)S(1)} %get-tuple-element.29), channel_id=1, source_target_pairs={{0,64},{1,65},{2,66},{3,67},{4,68},{5,69},{6,70},{7,71},{8,72},{9,... | collective-permute-start | bytes 393224 | tf_op jit(solution)/shard_map/ppermute | solution.py:62
  96.1 15.7 %collective-permute-start.1 = (f32[64,512]{0,1:T(8,128)S(1)}, f32[64,512]{0,1:T(8,128)}, u32[]{:S(2)}, u32[]{:S(2)}) collective-permute-start(f32[64,512]{0,1:T(8,128)S(1)} %get-tuple-element.23), channel_id=1, source_target_pairs={{0,32},{1,33},{2,34},{3,35},{4,36},{5,37},{6,38},{7,39},{8,40},{9,... | collective-permute-start | bytes 393224 | tf_op jit(solution)/shard_map/ppermute | solution.py:62
  113.3 25.5 %collective-permute-start.8 = (f32[64,512]{0,1:T(8,128)S(1)}, f32[64,512]{0,1:T(8,128)S(1)}, u32[]{:S(2)}, u32[]{:S(2)}) collective-permute-start(f32[64,512]{0,1:T(8,128)S(1)} %fusion.38), channel_id=1, source_target_pairs={{0,0},{32,1},{64,2},{96,3},{128,4},{160,5},{192,6},{224,7},{1,8},{... | collective-permute-start | bytes 393224 | tf_op jit(solution)/shard_map/ppermute | solution.py:55
  182.7 18.8 %all-to-all-start.5 = ((f32[32,8,768]{2,1,0:T(8,128)}), f32[32,8,768]{2,1,0:T(8,128)S(1)}, u32[]{:S(2)}, u32[]{:S(2)}) async-start(f32[32,8,768]{2,1,0:T(8,128)} %tile.15), calls=%async_computation.5 | async-start | bytes 1572864 | tf_op jit(solution)/shard_map/all_to_all | solution.py:37
  201.5 60.3 %copy-start.5 = (f32[32,8,768]{2,1,0:T(8,128)}, f32[32,8,768]{2,1,0:T(8,128)S(1)}, u32[]{:S(2)}) copy-start(f32[32,8,768]{2,1,0:T(8,128)S(1)} %all-to-all-done.5) | copy-start | bytes 2359300
  271.8 22.6 %all-to-all-start.1 = ((f32[8,64,256]{2,1,0:T(8,128)}), f32[8,64,256]{2,1,0:T(8,128)S(1)}, u32[]{:S(2)}, u32[]{:S(2)}) async-start(f32[8,64,256]{2,1,0:T(8,128)} %bitcast.3), calls=%async_computation.1 | async-start | bytes 1048576 | tf_op jit(solution)/shard_map/all_to_all | solution.py:46
  295.7 16.7 %all-to-all-start.6 = ((f32[32,8,512]{2,1,0:T(8,128)}), f32[32,8,512]{2,1,0:T(8,128)S(1)}, u32[]{:S(2)}, u32[]{:S(2)}) async-start(f32[32,8,512]{2,1,0:T(8,128)} %maximum_bitcast_fusion.2), calls=%async_computation.6 | async-start | bytes 1048576 | tf_op jit(solution)/shard_map/all_to_all | solution.py:46
  313.1 13.1 %all-to-all-start.7 = ((f32[8,8,512]{2,1,0:T(8,128)}), f32[8,8,512]{2,1,0:T(8,128)S(1)}, u32[]{:S(2)}, u32[]{:S(2)}) async-start(f32[8,8,512]{2,1,0:T(8,128)} %tile.16), calls=%async_computation.7 | async-start | bytes 262144 | tf_op jit(solution)/shard_map/all_to_all | solution.py:37
  327.1 15.7 %all-to-all-start.8 = ((f32[32,8,512]{2,1,0:T(8,128)}), f32[32,8,512]{2,1,0:T(8,128)S(1)}, u32[]{:S(2)}, u32[]{:S(2)}) async-start(f32[32,8,512]{2,1,0:T(8,128)} %tile.17), calls=%async_computation.8 | async-start | bytes 1048576 | tf_op jit(solution)/shard_map/all_to_all | solution.py:37
  331.0 58.9 %all-gather.8.cloned.1.call-start = ((), (), s32[]{:S(2)}) async-start(), calls=%async_computation.11 | async-start | bytes 1769472 | tf_op jit(solution)/shard_map/all_gather | solution.py:97
  331.5 7.4 %collective-permute-start.9 = (f32[64,256]{1,0:T(8,128)S(1)}, f32[64,256]{1,0:T(8,128)S(1)}, u32[]{:S(2)}, u32[]{:S(2)}) collective-permute-start(f32[64,256]{1,0:T(8,128)S(1)} %reduce_sum.36), channel_id=1, source_target_pairs={{0,0},{32,1},{64,2},{96,3},{128,4},{160,5},{192,6},{224,7},{1,8},{... | collective-permute-start | bytes 196616 | tf_op jit(solution)/shard_map/ppermute | solution.py:55
  344.4 40.2 %all-to-all-start.2 = ((f32[32,64,256]{2,1,0:T(8,128)}), f32[32,64,256]{2,1,0:T(8,128)}, u32[]{:S(2)}, u32[]{:S(2)}) async-start(f32[32,64,256]{2,1,0:T(8,128)} %stack.2), calls=%async_computation.2 | async-start | bytes 4194304 | tf_op jit(solution)/shard_map/all_to_all | solution.py:95
  389.9 5.2 %copy-start.4 = (f32[2048,256]{0,1:T(8,128)S(1)}, f32[2048,256]{0,1:T(8,128)}, u32[]{:S(2)}) copy-start(f32[2048,256]{0,1:T(8,128)} %fusion.7) | copy-start | bytes 6291460
  (9 other events, 22.8 us)
Sparse Core Ops, SparseCore 0:
  10.6 57.5 all-gather.3
  139.8 54.1 all-gather.5
  336.2 35.3 all-gather.7
